TPU v7x, 32 devices: a whole 2x2x4 slice. The times are simulated.
32 devices in a mesh: vox: 4 (over x, core), mem: 8 (over z, y).
Axes of the slice: x: 2, y: 2, z: 4, core: 2. Of those that a mesh axis runs over, the one named last changes fastest.
Arguments:
- ensemble: bfloat16 [256, 65536], P('mem', 'vox'), may hold values from -6 to 6
- partials: float32 [4, 256, 16384], P('vox', 'mem'), may hold values from -6 to 6
- perturb: float32 [256, 16384], P('mem', 'vox'), may hold values from -6 to 6
- observed: float32 [16384], P('vox'), may hold values from -6 to 6
- variance: float32 [16384], P('vox'), may hold values from 0.5 to 2
- obs_lists: int32 [512, 16], P(('vox', 'mem')), may hold values from 0 to 31, all different within a row
- taper_index: int32 [512, 16], P(('vox', 'mem')), may hold values from 0 to 15
- taper_table: float32 [16], replicated, may hold values from 0.1 to 1
Outputs:
- updated: bfloat16 [256, 65536], P('mem', 'vox')
All inputs are finite; a program needn't handle non-finite values.
Results may differ from a plain program's by a relative error of at most 0.017.
Values may be sent and summed in bfloat16 or wider, within the bound.
No kernel may reach another device: no remote copies, remote signals or barrier semaphores. Data moves between devices by JAX's collectives and lax.ppermute only.
A program may use at most 128 MiB of HBM per device.

v0:
```python
import jax
import jax.numpy as jnp
from jax import lax
from jax.sharding import PartitionSpec as P

OB = 128


def center(values):
    as_float = values.astype(jnp.float32)
    return (as_float - jnp.mean(as_float, axis=0, keepdims=True)).astype(jnp.bfloat16)


def block_moments(obs_anom, weights):
    return jnp.einsum("kbi,lbi->bkl", obs_anom, weights, preferred_element_type=jnp.float32)


def from_moments(moments, coeff, state_anom):
    high = lax.Precision.HIGHEST
    combined = jnp.einsum("bo,okl->bkl", coeff, moments, precision=high).astype(jnp.bfloat16)
    return jnp.einsum("kbc,bkl->lbc", state_anom, combined, preferred_element_type=jnp.float32)


def local(ensemble, partials, perturb, observed, variance, obs_lists, taper_index, taper_table):
    summed = lax.psum_scatter(
        partials[0].astype(jnp.bfloat16), "vox", scatter_dimension=1, tiled=True
    )
    weights = (
        (observed[None, :] + perturb - summed.astype(jnp.float32)) / variance[None, :]
    ).astype(jnp.bfloat16)
    members = lax.all_to_all(ensemble, "mem", split_axis=1, concat_axis=0, tiled=True)
    count = members.shape[0]
    blocks = obs_lists.shape[0]
    cells = members.shape[1] // blocks
    groups = weights.shape[1] // OB
    state_anom = center(members).reshape(count, blocks, cells)
    table_hits = (
        taper_index[:, :, None] == jnp.arange(taper_table.shape[0], dtype=jnp.int32)[None, None, :]
    ).astype(jnp.float32)
    tapers = jnp.sum(table_hits * taper_table[None, None, :], axis=2)
    picks = (obs_lists[:, :, None] == jnp.arange(groups, dtype=jnp.int32)[None, None, :]).astype(
        jnp.float32
    )
    coeff = jnp.sum(tapers[:, :, None] * picks, axis=1)
    pred_own, wts_own = (
        lax.all_to_all(summed, "mem", split_axis=1, concat_axis=0, tiled=True),
        lax.all_to_all(weights, "mem", split_axis=1, concat_axis=0, tiled=True),
    )
    own_anom = center(pred_own).reshape(count, -1, OB)
    own_moments = block_moments(own_anom, wts_own.reshape(count, -1, OB))
    moments = lax.all_gather(own_moments.astype(jnp.bfloat16), "mem", axis=0, tiled=True).astype(
        own_moments.dtype
    )
    increment = from_moments(moments, coeff, state_anom).reshape(count, blocks * cells)
    updated = (members.astype(jnp.float32) + increment * (1.0 / (count - 1))).astype(jnp.bfloat16)
    return lax.all_to_all(updated, "mem", split_axis=0, concat_axis=1, tiled=True)


def solution(mesh):
    return jax.shard_map(
        local,
        mesh=mesh,
        in_specs=(
            P("mem", "vox"),
            P("vox", "mem", None),
            P("mem", "vox"),
            P("vox"),
            P("vox"),
            P(("vox", "mem"), None),
            P(("vox", "mem"), None),
            P(),
        ),
        out_specs=P("mem", "vox"),
        check_vma=False,
    )
```

profile of v0, /device:TPU:0, one launch (start us, length us, event | category | flops | bytes accessed | tf_op | source)
XLA Modules:
  0.0 203.3 jit_solution(8342497593390177636)
XLA Ops:
  6.5 2.7 %convert_bitcast_fusion = bf16[32,16384]{1,0:T(8,128)(2,1)} fusion(f32[1,32,16384]{2,1,0:T(8,128)} %param.9), kind=kLoop, calls=%fused_computation.13 | loop fusion | flops 524288 | bytes 3145728 | tf_op jit(solution)/shard_map/convert_element_type | solution.py:26
  9.3 28.1 %reduce-scatter.2.cloned.1.call-done = bf16[32,4096]{1,0:T(8,128)(2,1)} async-done(((bf16[32,16384]{1,0:T(8,128)(2,1)}), bf16[32,4096]{1,0:T(8,128)(2,1)}) %reduce-scatter.2.cloned.1.call-update) | async-done | bytes 262160 | tf_op jit(solution)/shard_map/reduce_scatter | solution.py:25
  37.4 1.7 copy.67
  39.1 5.5 %all-to-all-start.1 = ((bf16[32,8,512]{2,0,1:T(8,128)(2,1)}), bf16[32,8,512]{2,0,1:T(8,128)(2,1)S(1)}, u32[]{:S(2)}, u32[]{:S(2)}) async-start(bf16[32,8,512]{2,0,1:T(8,128)(2,1)} %bitcast.38), calls=%async_computation.2 | async-start | bytes 524288 | tf_op jit(solution)/shard_map/all_to_all | solution.py:46
  44.6 1.0 divide_convert_fusion
  45.7 0.7 copy.66
  46.4 7.0 %all-to-all-done.1 = bf16[32,8,512]{2,0,1:T(8,128)(2,1)S(1)} async-done(((bf16[32,8,512]{2,0,1:T(8,128)(2,1)}), bf16[32,8,512]{2,0,1:T(8,128)(2,1)S(1)}, u32[]{:S(2)}, u32[]{:S(2)}) %all-to-all-start.1) | async-done | bytes 262176 | tf_op jit(solution)/shard_map/all_to_all | solution.py:46
  53.3 3.6 %all-to-all-start.2 = ((bf16[32,8,512]{2,0,1:T(8,128)(2,1)}), bf16[32,8,512]{2,0,1:T(8,128)(2,1)S(1)}, u32[]{:S(2)}, u32[]{:S(2)}) async-start(bf16[32,8,512]{2,0,1:T(8,128)(2,1)} %bitcast.37), calls=%async_computation.3 | async-start | bytes 524288 | tf_op jit(solution)/shard_map/all_to_all | solution.py:47
  57.0 0.1 convert_bitcast_fusion.1
  57.0 0.2 reshape.60
  57.2 0.1 convert_reduce_fusion.1
  57.3 8.2 %all-to-all-done.2 = bf16[32,8,512]{2,0,1:T(8,128)(2,1)S(1)} async-done(((bf16[32,8,512]{2,0,1:T(8,128)(2,1)}), bf16[32,8,512]{2,0,1:T(8,128)(2,1)S(1)}, u32[]{:S(2)}, u32[]{:S(2)}) %all-to-all-start.2) | async-done | bytes 262176 | tf_op jit(solution)/shard_map/all_to_all | solution.py:47
  65.5 0.1 reshape.59
  65.6 0.1 subtract_convert_fusion
  65.7 1.1 convolution_convert_fusion
  66.9 1.0 copy.65
  67.9 3.6 %all-to-all-start = ((bf16[32,8,2048]{2,0,1:T(8,128)(2,1)}), bf16[32,8,2048]{2,0,1:T(8,128)(2,1)S(1)}, u32[]{:S(2)}, u32[]{:S(2)}) async-start(bf16[32,8,2048]{2,0,1:T(8,128)(2,1)} %bitcast.36), calls=%async_computation | async-start | bytes 2097152 | tf_op jit(solution)/shard_map/all_to_all | solution.py:31
  71.5 0.2 select_reduce_fusion.1
  71.7 0.1 select_reduce_fusion
  71.9 42.0 %all-to-all-done = bf16[32,8,2048]{2,0,1:T(8,128)(2,1)S(1)} async-done(((bf16[32,8,2048]{2,0,1:T(8,128)(2,1)}), bf16[32,8,2048]{2,0,1:T(8,128)(2,1)S(1)}, u32[]{:S(2)}, u32[]{:S(2)}) %all-to-all-start) | async-done | bytes 1048608 | tf_op jit(solution)/shard_map/all_to_all | solution.py:31
  113.9 0.2 convert_element_type.65
  114.1 0.4 copy.47
  114.5 0.2 convert_reduce_fusion
  114.7 0.2 fusion.2
  114.9 39.9 %all-gather.2.cloned.1.call-done = bf16[32,256,256]{2,1,0:T(8,128)(2,1)} async-done(((bf16[4,256,256]{2,1,0:T(8,128)(2,1)}), bf16[32,256,256]{2,1,0:T(8,128)(2,1)}) %all-gather.2.cloned.1.call-update) | async-done | bytes 4194320 | tf_op jit(solution)/shard_map/all_gather | solution.py:51
  154.8 5.8 %fusion.6 = bf16[16,256,256]{2,0,1:T(8,128)(2,1)S(1)} fusion(bf16[32,256,256]{2,1,0:T(8,128)(2,1)} %all-gather.2.cloned.1.call-done, f32[16,32]{1,0:T(8,128)S(1)} %select_reduce_fusion), kind=kOutput, calls=%fused_computation.9 | convolution fusion | flops 403701760 | bytes 6293504 | tf_op jit(solution)/shard_map/bo,okl->bkl/dot_general | solution.py:20
  160.5 1.7 multiply_bitcast_fusion
  162.2 2.5 %copy.41 = f32[256,16,128]{2,1,0:T(8,128)} copy(f32[256,16,128]{2,0,1:T(8,128)S(1)} %multiply_bitcast_fusion) | data formatting | bytes 4194304 | tf_op jit(solution)/shard_map/mul | solution.py:55
  164.8 1.7 mul.36
  166.5 0.3 fusion.3
  166.8 28.7 %all_to_all.58 = bf16[8,32,2048]{2,1,0:T(8,128)(2,1)S(1)} all-to-all(bf16[8,32,2048]{2,1,0:T(8,128)(2,1)S(1)} %fusion.3), channel_id=1, replica_groups=mesh['vox'=4,'mem'=8] {'mem'}, dimensions={0} | all-to-all | bytes 2097152 | tf_op jit(solution)/shard_map/all_to_all | solution.py:56
  195.4 1.0 copy.46
  (20 shorter events, 0.1 us)
Async XLA Ops:
  6.5 38.1 %copy-start.1 = (f32[32,4096]{1,0:T(8,128)S(1)}, f32[32,4096]{1,0:T(8,128)}, u32[]{:S(2)}) copy-start(f32[32,4096]{1,0:T(8,128)} %param.10) | copy-start | bytes 1572868
  6.5 38.1 %copy-start.3 = (f32[4096]{0:T(1024)S(1)}, f32[4096]{0:T(1024)}, u32[]{:S(2)}) copy-start(f32[4096]{0:T(1024)} %param.11) | copy-start | bytes 49156
  6.5 38.1 %copy-start.2 = (f32[4096]{0:T(1024)S(1)}, f32[4096]{0:T(1024)}, u32[]{:S(2)}) copy-start(f32[4096]{0:T(1024)} %param.12) | copy-start | bytes 49156
  6.5 30.9 %reduce-scatter.2.cloned.1.call-start = ((), (), s32[]{:S(2)}) async-start(), calls=%async_computation.5 | async-start | bytes 1310720 | tf_op jit(solution)/shard_map/reduce_scatter | solution.py:25
  39.1 14.3 %all-to-all-start.1 = ((bf16[32,8,512]{2,0,1:T(8,128)(2,1)}), bf16[32,8,512]{2,0,1:T(8,128)(2,1)S(1)}, u32[]{:S(2)}, u32[]{:S(2)}) async-start(bf16[32,8,512]{2,0,1:T(8,128)(2,1)} %bitcast.38), calls=%async_computation.2 | async-start | bytes 524288 | tf_op jit(solution)/shard_map/all_to_all | solution.py:46
  53.3 12.2 %all-to-all-start.2 = ((bf16[32,8,512]{2,0,1:T(8,128)(2,1)}), bf16[32,8,512]{2,0,1:T(8,128)(2,1)S(1)}, u32[]{:S(2)}, u32[]{:S(2)}) async-start(bf16[32,8,512]{2,0,1:T(8,128)(2,1)} %bitcast.37), calls=%async_computation.3 | async-start | bytes 524288 | tf_op jit(solution)/shard_map/all_to_all | solution.py:47
  56.9 97.8 %all-gather.2.cloned.1.call-start = ((), (), s32[]{:S(2)}) async-start(), calls=%async_computation.6 | async-start | bytes 4718592 | tf_op jit(solution)/shard_map/all_gather | solution.py:51
  57.0 9.8 %copy-start = (bf16[32,16384]{1,0:T(8,128)(2,1)S(1)}, bf16[32,16384]{1,0:T(8,128)(2,1)}, u32[]{:S(2)}) copy-start(bf16[32,16384]{1,0:T(8,128)(2,1)} %param.8) | copy-start | bytes 3145732
  66.8 4.7 %copy-start.5 = (s32[16,16]{1,0:T(8,128)S(1)}, s32[16,16]{1,0:T(8,128)}, u32[]{:S(2)}) copy-start(s32[16,16]{1,0:T(8,128)} %param.14) | copy-start | bytes 3076
  66.8 4.7 %copy-start.6 = (f32[16]{0:T(128)S(1)}, f32[16]{0:T(128)}, u32[]{:S(2)}) copy-start(f32[16]{0:T(128)} %param.15) | copy-start | bytes 196
  66.8 4.9 %copy-start.4 = (s32[16,16]{1,0:T(8,128)S(1)}, s32[16,16]{1,0:T(8,128)}, u32[]{:S(2)}) copy-start(s32[16,16]{1,0:T(8,128)} %param.13) | copy-start | bytes 3076
  67.9 46.0 %all-to-all-start = ((bf16[32,8,2048]{2,0,1:T(8,128)(2,1)}), bf16[32,8,2048]{2,0,1:T(8,128)(2,1)S(1)}, u32[]{:S(2)}, u32[]{:S(2)}) async-start(bf16[32,8,2048]{2,0,1:T(8,128)(2,1)} %bitcast.36), calls=%async_computation | async-start | bytes 2097152 | tf_op jit(solution)/shard_map/all_to_all | solution.py:31
Sparse Core Ops, SparseCore 0:
  9.9 27.4 reduce-scatter.1
  66.9 87.7 all-gather.1
where the time goes:
time: 204 us; the launch traced here: 203 us
  waiting for transfers between devices  125 us (61%)
  blocking collectives  28.7 us (14%)
  between operations  13.6 us (7%)
  starting transfers between devices  12.7 us (6%)
  local copies, waits for them, and re-layouts  9.4 us (5%)
  matrix products  8.55 us (4%)
  other arithmetic  5.17 us (3%)
    all_to_all x1, waiting for transfers between devices, local(): lax.all_to_all(ensemble, 'mem', split_axis=1, concat_axis=0, tiled=True)  42 us
    all_gather x1, waiting for transfers between devices, local(): lax.all_gather(own_moments.astype(jnp.bfloat16), 'mem', axis=0, tiled=True)  39.9 us
    all_to_all x1, blocking collectives, local(): lax.all_to_all(updated, 'mem', split_axis=0, concat_axis=1, tiled=True)  28.7 us
    reduce_scatter x1, waiting for transfers between devices, local(): lax.psum_scatter(partials[0].astype(jnp.bfloat16), 'vox', scatter_dimensi...  28.1 us
    all_to_all x1, waiting for transfers between devices, local(): lax.all_to_all(weights, 'mem', split_axis=1, concat_axis=0, tiled=True)  8.19 us
    all_to_all x1, waiting for transfers between devices, local(): lax.all_to_all(summed, 'mem', split_axis=1, concat_axis=0, tiled=True)  6.96 us
    dot_general x1, matrix products, from_moments(): jnp.einsum('bo,okl->bkl', coeff, moments, precision=high)  5.77 us
    all_to_all x1, starting transfers between devices, local(): lax.all_to_all(summed, 'mem', split_axis=1, concat_axis=0, tiled=True)  5.52 us
  transfers between devices with their start and end apart: 5, of which 5 were waited for; matrix products, arithmetic and copies ran while one was open for 2% of the time, Pallas kernels for 0%

commit v1 on v0

--- a/solution.py
+++ b/solution.py
@@ -43,7 +43,10 @@
     )
     coeff = jnp.sum(tapers[:, :, None] * picks, axis=1)
     pred_own, wts_own = (
-        lax.all_to_all(summed, "mem", split_axis=1, concat_axis=0, tiled=True),
+        jnp.concatenate(
+            lax.all_to_all(jnp.stack(jnp.split(summed, lax.axis_size("mem"), axis=1)), "mem", 0, 0),
+            axis=0,
+        ),
         lax.all_to_all(weights, "mem", split_axis=1, concat_axis=0, tiled=True),
     )
     own_anom = center(pred_own).reshape(count, -1, OB)

time: 204 us -> 214 us (1.049)
  local copies, waits for them, and re-layouts: 9.4 us -> 18.7 us
    unnamed x15 -> x22, local copies, waits for them, and re-layouts: 0.42 us -> 10 us
where the time goes in v1:
time: 214 us; the launch traced here: 213 us
  waiting for transfers between devices  125 us (58%)
  blocking collectives  28.7 us (13%)
  local copies, waits for them, and re-layouts  18.7 us (9%)
  between operations  13.6 us (6%)
  starting transfers between devices  12.7 us (6%)
  matrix products  8.56 us (4%)
  other arithmetic  5.03 us (2%)
    all_to_all x1, waiting for transfers between devices, local(): lax.all_to_all(ensemble, 'mem', split_axis=1, concat_axis=0, tiled=True)  42 us
    all_gather x1, waiting for transfers between devices, local(): lax.all_gather(own_moments.astype(jnp.bfloat16), 'mem', axis=0, tiled=True)  39.9 us
    all_to_all x1, blocking collectives, local(): lax.all_to_all(updated, 'mem', split_axis=0, concat_axis=1, tiled=True)  28.7 us
    reduce_scatter x1, waiting for transfers between devices, local(): lax.psum_scatter(partials[0].astype(jnp.bfloat16), 'vox', scatter_dimensi...  28.1 us
    unnamed x22, local copies, waits for them, and re-layouts  10 us
    all_to_all x1, waiting for transfers between devices, local(): lax.all_to_all(weights, 'mem', split_axis=1, concat_axis=0, tiled=True)  8.45 us
    all_to_all x1, waiting for transfers between devices, local(): lax.all_to_all(jnp.stack(jnp.split(summed, lax.axis_size('mem'), axis=1))...  6.97 us
    dot_general x1, matrix products, from_moments(): jnp.einsum('bo,okl->bkl', coeff, moments, precision=high)  5.77 us
  transfers between devices with their start and end apart: 5, of which 5 were waited for; matrix products, arithmetic and copies ran while one was open for 2% of the time, Pallas kernels for 0%

profile of v1, /device:TPU:0, one launch (start us, length us, event | category | flops | bytes accessed | tf_op | source)
XLA Modules:
  0.0 212.7 jit_solution(7133624367926183861)
XLA Ops:
  6.5 2.7 %convert_bitcast_fusion = bf16[32,16384]{1,0:T(8,128)(2,1)} fusion(f32[1,32,16384]{2,1,0:T(8,128)} %param.9), kind=kLoop, calls=%fused_computation.13 | loop fusion | flops 524288 | bytes 3145728 | tf_op jit(solution)/shard_map/convert_element_type | solution.py:26
  9.3 28.1 %reduce-scatter.2.cloned.1.call-done = bf16[32,4096]{1,0:T(8,128)(2,1)} async-done(((bf16[32,16384]{1,0:T(8,128)(2,1)}), bf16[32,4096]{1,0:T(8,128)(2,1)}) %reduce-scatter.2.cloned.1.call-update) | async-done | bytes 262160 | tf_op jit(solution)/shard_map/reduce_scatter | solution.py:25
  37.4 1.4 fusion.23
  38.8 1.4 fusion.22
  40.1 1.4 fusion.21
  41.5 1.4 fusion.20
  42.9 1.4 fusion.19
  44.3 1.4 fusion.18
  45.6 1.4 fusion.17
  47.0 1.4 fusion.16
  48.4 5.5 %all-to-all-start.1 = ((bf16[8,32,512]{2,1,0:T(8,128)(2,1)}), bf16[8,32,512]{2,1,0:T(8,128)(2,1)S(1)}, u32[]{:S(2)}, u32[]{:S(2)}) async-start(bf16[8,32,512]{2,1,0:T(8,128)(2,1)} %fusion.16), calls=%async_computation.2 | async-start | bytes 524288 | tf_op jit(solution)/shard_map/all_to_all | solution.py:47
  53.9 1.0 divide_convert_fusion
  55.0 0.7 copy.62
  55.7 7.0 %all-to-all-done.1 = bf16[8,32,512]{2,1,0:T(8,128)(2,1)S(1)} async-done(((bf16[8,32,512]{2,1,0:T(8,128)(2,1)}), bf16[8,32,512]{2,1,0:T(8,128)(2,1)S(1)}, u32[]{:S(2)}, u32[]{:S(2)}) %all-to-all-start.1) | async-done | bytes 262176 | tf_op jit(solution)/shard_map/all_to_all | solution.py:47
  62.7 3.6 %all-to-all-start.2 = ((bf16[32,8,512]{2,0,1:T(8,128)(2,1)}), bf16[32,8,512]{2,0,1:T(8,128)(2,1)S(1)}, u32[]{:S(2)}, u32[]{:S(2)}) async-start(bf16[32,8,512]{2,0,1:T(8,128)(2,1)} %bitcast.64), calls=%async_computation.3 | async-start | bytes 524288 | tf_op jit(solution)/shard_map/all_to_all | solution.py:50
  66.4 8.4 %all-to-all-done.2 = bf16[32,8,512]{2,0,1:T(8,128)(2,1)S(1)} async-done(((bf16[32,8,512]{2,0,1:T(8,128)(2,1)}), bf16[32,8,512]{2,0,1:T(8,128)(2,1)S(1)}, u32[]{:S(2)}, u32[]{:S(2)}) %all-to-all-start.2) | async-done | bytes 262176 | tf_op jit(solution)/shard_map/all_to_all | solution.py:50
  75.1 1.1 convolution_convert_fusion
  76.3 1.0 copy.61
  77.3 3.6 %all-to-all-start = ((bf16[32,8,2048]{2,0,1:T(8,128)(2,1)}), bf16[32,8,2048]{2,0,1:T(8,128)(2,1)S(1)}, u32[]{:S(2)}, u32[]{:S(2)}) async-start(bf16[32,8,2048]{2,0,1:T(8,128)(2,1)} %bitcast.63), calls=%async_computation | async-start | bytes 2097152 | tf_op jit(solution)/shard_map/all_to_all | solution.py:31
  80.9 0.2 select_reduce_fusion.1
  81.3 42.0 %all-to-all-done = bf16[32,8,2048]{2,0,1:T(8,128)(2,1)S(1)} async-done(((bf16[32,8,2048]{2,0,1:T(8,128)(2,1)}), bf16[32,8,2048]{2,0,1:T(8,128)(2,1)S(1)}, u32[]{:S(2)}, u32[]{:S(2)}) %all-to-all-start) | async-done | bytes 1048608 | tf_op jit(solution)/shard_map/all_to_all | solution.py:31
  123.3 0.2 convert_element_type.61
  123.5 0.4 copy.42
  124.1 0.2 fusion.2
  124.3 39.9 %all-gather.2.cloned.1.call-done = bf16[32,256,256]{2,1,0:T(8,128)(2,1)} async-done(((bf16[4,256,256]{2,1,0:T(8,128)(2,1)}), bf16[32,256,256]{2,1,0:T(8,128)(2,1)}) %all-gather.2.cloned.1.call-update) | async-done | bytes 4194320 | tf_op jit(solution)/shard_map/all_gather | solution.py:54
  164.2 5.8 %fusion.6 = bf16[16,256,256]{2,0,1:T(8,128)(2,1)S(1)} fusion(bf16[32,256,256]{2,1,0:T(8,128)(2,1)} %all-gather.2.cloned.1.call-done, f32[16,32]{1,0:T(8,128)S(1)} %select_reduce_fusion), kind=kOutput, calls=%fused_computation.9 | convolution fusion | flops 403701760 | bytes 6293504 | tf_op jit(solution)/shard_map/bo,okl->bkl/dot_general | solution.py:20
  169.9 1.7 multiply_bitcast_fusion
  171.6 2.5 %copy.37 = f32[256,16,128]{2,1,0:T(8,128)} copy(f32[256,16,128]{2,0,1:T(8,128)S(1)} %multiply_bitcast_fusion) | data formatting | bytes 4194304 | tf_op jit(solution)/shard_map/mul | solution.py:58
  174.2 1.7 mul.36
  175.9 0.3 fusion.3
  176.2 28.7 %all_to_all.50 = bf16[8,32,2048]{2,1,0:T(8,128)(2,1)S(1)} all-to-all(bf16[8,32,2048]{2,1,0:T(8,128)(2,1)S(1)} %fusion.3), channel_id=1, replica_groups=mesh['vox'=4,'mem'=8] {'mem'}, dimensions={0} | all-to-all | bytes 2097152 | tf_op jit(solution)/shard_map/all_to_all | solution.py:59
  204.8 1.0 copy.41
  (25 shorter events, 0.7 us)
Async XLA Ops:
  6.5 47.4 %copy-start.1 = (f32[32,4096]{1,0:T(8,128)S(1)}, f32[32,4096]{1,0:T(8,128)}, u32[]{:S(2)}) copy-start(f32[32,4096]{1,0:T(8,128)} %param.10) | copy-start | bytes 1572868
  6.5 47.4 %copy-start.3 = (f32[4096]{0:T(1024)S(1)}, f32[4096]{0:T(1024)}, u32[]{:S(2)}) copy-start(f32[4096]{0:T(1024)} %param.11) | copy-start | bytes 49156
  6.5 47.4 %copy-start.2 = (f32[4096]{0:T(1024)S(1)}, f32[4096]{0:T(1024)}, u32[]{:S(2)}) copy-start(f32[4096]{0:T(1024)} %param.12) | copy-start | bytes 49156
  6.5 30.9 %reduce-scatter.2.cloned.1.call-start = ((), (), s32[]{:S(2)}) async-start(), calls=%async_computation.5 | async-start | bytes 1310720 | tf_op jit(solution)/shard_map/reduce_scatter | solution.py:25
  48.4 14.3 %all-to-all-start.1 = ((bf16[8,32,512]{2,1,0:T(8,128)(2,1)}), bf16[8,32,512]{2,1,0:T(8,128)(2,1)S(1)}, u32[]{:S(2)}, u32[]{:S(2)}) async-start(bf16[8,32,512]{2,1,0:T(8,128)(2,1)} %fusion.16), calls=%async_computation.2 | async-start | bytes 524288 | tf_op jit(solution)/shard_map/all_to_all | solution.py:47
  55.7 20.5 %copy-start = (bf16[32,16384]{1,0:T(8,128)(2,1)S(1)}, bf16[32,16384]{1,0:T(8,128)(2,1)}, u32[]{:S(2)}) copy-start(bf16[32,16384]{1,0:T(8,128)(2,1)} %param.8) | copy-start | bytes 3145732
  62.7 12.2 %all-to-all-start.2 = ((bf16[32,8,512]{2,0,1:T(8,128)(2,1)}), bf16[32,8,512]{2,0,1:T(8,128)(2,1)S(1)}, u32[]{:S(2)}, u32[]{:S(2)}) async-start(bf16[32,8,512]{2,0,1:T(8,128)(2,1)} %bitcast.64), calls=%async_computation.3 | async-start | bytes 524288 | tf_op jit(solution)/shard_map/all_to_all | solution.py:50
  66.3 97.9 %all-gather.2.cloned.1.call-start = ((), (), s32[]{:S(2)}) async-start(), calls=%async_computation.6 | async-start | bytes 4718592 | tf_op jit(solution)/shard_map/all_gather | solution.py:54
  76.2 4.7 %copy-start.5 = (s32[16,16]{1,0:T(8,128)S(1)}, s32[16,16]{1,0:T(8,128)}, u32[]{:S(2)}) copy-start(s32[16,16]{1,0:T(8,128)} %param.14) | copy-start | bytes 3076
  76.2 4.7 %copy-start.6 = (f32[16]{0:T(128)S(1)}, f32[16]{0:T(128)}, u32[]{:S(2)}) copy-start(f32[16]{0:T(128)} %param.15) | copy-start | bytes 196
  76.3 4.8 %copy-start.4 = (s32[16,16]{1,0:T(8,128)S(1)}, s32[16,16]{1,0:T(8,128)}, u32[]{:S(2)}) copy-start(s32[16,16]{1,0:T(8,128)} %param.13) | copy-start | bytes 3076
  77.3 46.0 %all-to-all-start = ((bf16[32,8,2048]{2,0,1:T(8,128)(2,1)}), bf16[32,8,2048]{2,0,1:T(8,128)(2,1)S(1)}, u32[]{:S(2)}, u32[]{:S(2)}) async-start(bf16[32,8,2048]{2,0,1:T(8,128)(2,1)} %bitcast.63), calls=%async_computation | async-start | bytes 2097152 | tf_op jit(solution)/shard_map/all_to_all | solution.py:31
Sparse Core Ops, SparseCore 0:
  9.9 27.4 reduce-scatter.1
  76.3 87.7 all-gather.1
